TPU v7x, 32 devices: a whole 2x2x4 slice. The times are simulated.
32 devices in a mesh: rad: 8 (over z, y), mode: 4 (over x, core).
Axes of the slice: x: 2, y: 2, z: 4, core: 2. Of those that a mesh axis runs over, the one named last changes fastest.
Arguments:
- coefficients: bfloat16 [3, 2, 256, 8, 4, 1152], P(None, None, 'rad', None, 'mode'), may hold values from -6 to 6
- legendre: bfloat16 [8, 4, 1152, 2048], P('rad', 'mode'), may hold values from -0.25 to 0.25
- radial_left_factor: float32 [3, 256, 256], replicated, may hold values from -0.375 to 0.375
- radial_right: float32 [3, 256, 256], replicated, may hold values from -0.375 to 0.375
- eigen_rates: float32 [3, 256], replicated, may hold values from 0.02 to 4
- diffusivity: float32 [3], replicated, may hold values from 0.5 to 4
- slot_order: int32 [8, 4, 2], P('rad', 'mode'), may hold values from 0 to 1023, as said below
- slot_start: int32 [8, 4, 2], P('rad', 'mode'), may hold values from 0 to 1024, as said below
Outputs:
- physical: bfloat16 [3, 2, 8, 4, 256, 2, 2048], P(None, None, None, None, 'rad', None, 'mode')
Inputs may be any that keep to these rules, and one draw needn't show every extreme that they name: `slot_order`: the 64 orders are distinct, 0 and 1023 among them; the two rows of every group have block counts 1024 / 128 - floor(m / 128) that add up to exactly 9. `slot_start`: in every group the first row starts at slot 0 and the second at 128 times the first row's block count.
All inputs are finite; a program needn't handle non-finite values.
Results may differ from a plain program's by a relative error of at most 0.0049.
Values may be sent and summed in bfloat16 or wider, within the bound.
A program may use at most 256 MiB of HBM per device.

v0:
```python
import jax
import jax.numpy as jnp
from jax import lax
from jax.sharding import PartitionSpec as P

DEGREES = 1024
BLOCK = 128
RADII = 256
LATS = 2048
PACKED = 1152


def slot_layout(orders, begin_offsets):
    position = jnp.arange(PACKED, dtype=jnp.int32)
    first_degree = BLOCK * (orders // BLOCK)
    row_length = DEGREES - first_degree
    inside = (position[None, :] >= begin_offsets[:, None]) & (
        position[None, :] < begin_offsets[:, None] + row_length[:, None]
    )
    degree_rows = first_degree[:, None] + position[None, :] - begin_offsets[:, None]
    active_mask = inside & (degree_rows >= orders[:, None])
    degree = jnp.sum(jnp.where(inside, degree_rows, 0), axis=0)
    return (active_mask, degree)


def on_device(
    coefficients,
    legendre,
    radial_left_factor,
    radial_right,
    eigen_rates,
    diffusivity,
    slot_order,
    slot_start,
):
    orders = slot_order.reshape(2)
    begin_offsets = slot_start.reshape(2)
    active_mask, degree = slot_layout(orders, begin_offsets)
    degree_level = degree.astype(jnp.float32)
    harmonic = degree_level * (degree_level + 1.0) / (DEGREES * DEGREES)
    shrink = 1.0 + eigen_rates[:, :, None] + diffusivity[:, None, None] * harmonic[None, None, :]
    covered = jnp.any(active_mask, axis=0).astype(jnp.float32)
    factor = covered[None, None, :] / shrink
    arrived = lax.all_to_all(coefficients, "rad", split_axis=3, concat_axis=2, tiled=True)
    parts_count = arrived.shape[1]
    field_values = arrived.reshape(3, parts_count, RADII, PACKED)
    per_field = []
    for field_index in range(3):
        per_part = []
        for part_index in range(parts_count):
            column_values = field_values[field_index, part_index].astype(jnp.float32)
            turned = jnp.dot(
                radial_left_factor[field_index], column_values, precision=lax.Precision.HIGHEST
            )
            scaled = turned * factor[field_index]
            result = jnp.dot(radial_right[field_index], scaled, precision=lax.Precision.HIGHEST)
            per_part.append(result.astype(jnp.bfloat16))
        per_field.append(jnp.stack(per_part, axis=0))
    updated = jnp.stack(per_field, axis=0).reshape(3, parts_count, RADII, 1, 1, PACKED)
    polynomial_rows = legendre.reshape(PACKED, LATS)
    row_masks = active_mask.astype(jnp.bfloat16)
    masked_rows = jnp.concatenate(
        [polynomial_rows * row_masks[0][:, None], polynomial_rows * row_masks[1][:, None]], axis=1
    )
    summed = jnp.dot(
        updated.reshape(6 * RADII, PACKED), masked_rows, preferred_element_type=jnp.float32
    )
    synthesized = summed.astype(jnp.bfloat16).reshape(3, 2, RADII, 2, LATS)
    sectioned = synthesized.reshape(3, 2, 1, 1, RADII, 2, LATS)
    physical = lax.all_to_all(
        lax.all_to_all(sectioned, "rad", split_axis=4, concat_axis=2, tiled=True),
        "mode",
        split_axis=6,
        concat_axis=3,
        tiled=True,
    )
    return physical


def solution(mesh):
    return jax.shard_map(
        on_device,
        mesh=mesh,
        in_specs=(
            P(None, None, "rad", None, "mode", None),
            P("rad", "mode", None, None),
            P(),
            P(),
            P(),
            P(),
            P("rad", "mode", None),
            P("rad", "mode", None),
        ),
        out_specs=P(None, None, None, None, "rad", None, "mode"),
        check_vma=False,
    )
```

profile of v0, /device:TPU:0, one launch (start us, length us, event | category | flops | bytes accessed | tf_op | source)
XLA Modules:
  0.0 865.9 jit_solution(206273658456439164)
XLA Ops:
  0.0 4.4 copy.22
  4.4 0.0 copy-start.2
  4.4 0.0 copy-start.4
  4.4 0.0 copy-start.3
  4.4 0.0 copy-start.5
  4.4 7.5 all-to-all-start
  11.9 0.0 copy-done.2
  11.9 0.0 copy-done.4
  11.9 0.1 fusion.36
  12.1 0.1 select_reduce_fusion
  12.2 0.0 copy-done.3
  12.2 0.0 copy-done.5
  12.2 0.1 broadcast_multiply_fusion
  12.3 0.5 add_divide_fusion
  12.8 6.7 bitcast_multiply_fusion.1
  19.5 71.6 %all-to-all-done = bf16[3,2,32,8,1,1152]{5,2,1,0,4,3:T(8,128)(2,1)} async-done(((bf16[3,2,32,8,1,1152]{5,2,1,0,4,3:T(8,128)(2,1)}), bf16[3,2,32,8,1,1152]{5,2,1,0,4,3:T(8,128)(2,1)}, u32[]{:S(2)}, u32[]{:S(2)}) %all-to-all-start) | async-done | bytes 3538976 | tf_op jit(solution)/shard_map/all_to_all | solution.py:44
  91.1 0.0 copy-start
  91.1 2.4 copy.23
  93.5 0.0 copy-done
  93.5 0.7 convolution_multiply_fusion
  94.2 0.7 convolution_multiply_fusion.1
  94.9 0.7 convolution_multiply_fusion.2
  95.6 0.7 convolution_multiply_fusion.3
  96.3 0.0 copy-start.1
  96.3 0.7 convolution_multiply_fusion.4
  97.0 0.7 convolution_multiply_fusion.5
  97.7 0.0 copy-done.1
  97.7 1.3 fusion.8
  99.0 1.3 fusion.7
  100.4 1.3 fusion.6
  101.7 1.3 fusion.5
  103.0 1.8 fusion.3
  104.8 0.0 slice-start
  104.8 0.0 slice-start.2
  104.8 1.3 fusion.4
  106.1 0.1 maximum_bitcast_fusion.2
  106.3 0.0 slice-start.1
  106.3 0.0 slice-start.3
  106.3 0.2 maximum_bitcast_fusion
  106.5 0.5 pad_maximum_fusion
  107.1 0.0 slice-done
  107.1 1.2 slice-done.2
  108.3 0.2 slice-done.1
  108.5 0.1 slice-done.3
  108.6 19.0 %convolution_convert_fusion = bf16[1536,4096]{1,0:T(8,128)(2,1)} fusion(bf16[1536,1152]{1,0:T(8,128)(2,1)S(1)} %bitcast.138, bf16[1152,2048]{1,0:T(8,128)(2,1)S(1)} %bitcast.137, bf16[1152,2048]{1,0:T(8,128)(2,1)S(1)} %bitcast.135), kind=kOutput, calls=%fused_computation | convolution fusion | flops 14520680448 | bytes 25559040 | tf_op jit(solution)/shard_map/dot_general | solution.py:65
  127.6 21.1 %reshape_reshape.7 = bf16[3,2,1,1,256,2,2048]{6,5,4,1,0,3,2:T(2,128)(2,1)} reshape(bf16[1536,4096]{1,0:T(8,128)(2,1)} %convolution_convert_fusion) | data formatting | bytes 25165824 | tf_op jit(solution)/shard_map/reshape;reshape | solution.py:69
  148.7 14.7 %copy.24 = bf16[3,2,1,1,256,2,2048]{6,5,1,0,3,2,4:T(2,128)(2,1)S(1)} copy(bf16[3,2,1,1,256,2,2048]{6,5,4,1,0,3,2:T(2,128)(2,1)} %reshape_reshape.7) | data formatting | bytes 25165824 | tf_op jit(solution)/shard_map/reshape;reshape | solution.py:69
  163.4 276.6 %all_to_all.45 = bf16[3,2,1,1,256,2,2048]{6,5,1,0,3,2,4:T(2,128)(2,1)} all-to-all(bf16[3,2,1,1,256,2,2048]{6,5,1,0,3,2,4:T(2,128)(2,1)S(1)} %copy.24), channel_id=1, replica_groups=mesh['rad'=8,'mode'=4] {'rad'}, dimensions={4} | all-to-all | bytes 25165824 | tf_op jit(solution)/shard_map/all_to_all | solution.py:71
  440.1 76.5 %copy.26 = bf16[3,2,8,1,32,2,2048]{4,2,5,1,0,3,6:T(8,128)(2,1)} copy(bf16[3,2,8,1,32,2,2048]{6,5,1,0,4,2,3:T(2,128)(2,1)} %bitcast.126) | data formatting | bytes 25165824 | tf_op jit(solution)/shard_map/all_to_all | solution.py:71
  516.6 71.7 %reshape.108 = bf16[4,2,786432]{2,1,0:T(2,128)(2,1)} reshape(bf16[2048,1,3,2,2,8,32]{6,5,4,3,2,1,0:T(8,128)(2,1)} %bitcast.124) | data formatting | bytes 25165824
  588.3 147.6 %all_to_all.46 = bf16[4,2,786432]{2,1,0:T(2,128)(2,1)} all-to-all(bf16[4,2,786432]{2,1,0:T(2,128)(2,1)} %reshape.108), channel_id=1, replica_groups=mesh['rad'=8,'mode'=4] {'mode'}, dimensions={0} | all-to-all | bytes 25165824 | tf_op jit(solution)/shard_map/all_to_all | solution.py:70
  735.9 52.0 %reshape.109 = bf16[2048,1,3,2,2,8,32]{6,5,4,3,2,1,0:T(8,128)(2,1)} reshape(bf16[4,2,786432]{2,1,0:T(2,128)(2,1)} %all_to_all.46) | data formatting | bytes 25165824
  787.9 54.0 %copy.31 = bf16[3,2,8,1,32,2,4,512]{7,6,4,5,2,1,0,3:T(4,128)(2,1)} copy(bf16[3,2,8,1,32,2,4,512]{4,2,5,1,0,7,6,3:T(8,128)(2,1)} %bitcast.125) | data formatting | bytes 25165824 | tf_op jit(solution)/shard_map/all_to_all | solution.py:70
  841.9 23.7 %copy.28 = bf16[3,2,8,4,32,2,512]{6,5,4,3,2,1,0:T(2,128)(2,1)} copy(bf16[3,2,8,4,32,2,512]{6,3,4,5,2,1,0:T(4,128)(2,1)} %bitcast.127) | data formatting | bytes 25165824 | tf_op jit(solution)/shard_map/all_to_all | solution.py:70
  (8 shorter events, 0.1 us)
Async XLA Ops:
  4.4 7.5 copy-start.2
  4.4 7.5 copy-start.4
  4.4 7.8 copy-start.3
  4.4 7.8 copy-start.5
  4.4 86.7 %all-to-all-start = ((bf16[3,2,32,8,1,1152]{5,2,1,0,4,3:T(8,128)(2,1)}), bf16[3,2,32,8,1,1152]{5,2,1,0,4,3:T(8,128)(2,1)}, u32[]{:S(2)}, u32[]{:S(2)}) async-start(bf16[3,2,32,8,1,1152]{5,2,1,0,4,3:T(8,128)(2,1)} %copy.22), calls=%async_computation | async-start | bytes 7077888 | tf_op jit(solution)/shard_map/all_to_all | solution.py:44
  91.1 2.4 copy-start
  96.3 1.4 copy-start.1
  104.8 2.3 slice-start
  104.8 3.5 slice-start.2
  106.3 2.2 slice-start.1
  106.3 2.4 slice-start.3
where the time goes:
time: 879 us; the launch traced here: 866 us
  blocking collectives  424 us (48%)
  local copies, waits for them, and re-layouts  322 us (37%)
  waiting for transfers between devices  71.6 us (8%)
  matrix products  31.5 us (4%)
    all_to_all x1, blocking collectives, on_device(): lax.all_to_all(sectioned, 'rad', split_axis=4, concat_axis=2, tiled=True)  277 us
    all_to_all x1, blocking collectives, on_device(): lax.all_to_all(lax.all_to_all(sectioned, 'rad', split_axis=4, concat_axis...  148 us
    unnamed x23, local copies, waits for them, and re-layouts  130 us
    all_to_all x2, local copies, waits for them, and re-layouts, on_device(): lax.all_to_all(lax.all_to_all(sectioned, 'rad', split_axis=4, concat_axis...  77.7 us
    all_to_all x1, local copies, waits for them, and re-layouts, on_device(): lax.all_to_all(sectioned, 'rad', split_axis=4, concat_axis=2, tiled=True)  76.5 us
    all_to_all x1, waiting for transfers between devices, on_device(): lax.all_to_all(coefficients, 'rad', split_axis=3, concat_axis=2, tiled=True)  71.6 us
    another operation x2, local copies, waits for them, and re-layouts, on_device(): sectioned = synthesized.reshape(3, 2, 1, 1, RADII, 2, LATS)  35.8 us
    dot_general x1, matrix products, on_device(): jnp.dot(updated.reshape(6 * RADII, PACKED), masked_rows, preferred_elemen...  19 us
  transfers between devices with their start and end apart: 1, of which 1 were waited for; matrix products, arithmetic and copies ran while one was open for 1% of the time, Pallas kernels for 0%

commit v1 on v0

v1 whole, which is shorter than its diff:
```python
import functools
import jax
import jax.numpy as jnp
from jax import lax
from jax.experimental import pallas as pl
from jax.experimental.pallas import tpu as pltpu
from jax.sharding import PartitionSpec as P

DEGREES = 1024
BLOCK = 128
MESH = pl.DeviceIdType.MESH


def slot_layout(orders, begin_offsets, packed):
    position = jnp.arange(packed, dtype=jnp.int32)
    first_degree = BLOCK * (orders // BLOCK)
    row_length = DEGREES - first_degree
    inside = (position[None, :] >= begin_offsets[:, None]) & (
        position[None, :] < begin_offsets[:, None] + row_length[:, None]
    )
    degree_rows = first_degree[:, None] + position[None, :] - begin_offsets[:, None]
    active_mask = inside & (degree_rows >= orders[:, None])
    degree = jnp.sum(jnp.where(inside, degree_rows, 0), axis=0)
    return (active_mask, degree)


def far_first(count):
    return sorted(range(count), key=lambda k: (-min(k, count - k), k))


def exchange_kernel(rads, modes, u_ref, l_ref, o_ref, held, send_sem, recv_sem, local_sem):
    my_rad = lax.axis_index("rad")
    my_mode = lax.axis_index("mode")
    devices = rads * modes
    parts = u_ref.shape[0]
    rows, lats = held.shape[1], held.shape[3]
    me = my_rad * modes + my_mode

    barrier = pltpu.get_barrier_semaphore()
    for ka in range(rads):
        for kb in range(modes):
            if ka or kb:
                peer = (lax.rem(my_rad + ka, rads), lax.rem(my_mode + kb, modes))
                pl.semaphore_signal(barrier, inc=1, device_id=peer, device_id_type=MESH)
    pl.semaphore_wait(barrier, devices - 1)

    def one_part(c, carry):
        for kb in range(modes):
            b = lax.rem(my_mode + kb, modes)
            columns = pl.ds(pl.multiple_of(b * lats, lats), lats)
            summed = jnp.dot(u_ref[c], l_ref[:, columns], preferred_element_type=jnp.float32)
            blocks = summed.reshape(rads, rows, 2, lats).astype(jnp.bfloat16)
            for a in range(rads):
                held[(c * modes + kb) * rads + a] = blocks[a]
            for ka in far_first(rads):
                a = lax.rem(my_rad + ka, rads)
                source = held.at[(c * modes + kb) * rads + a]
                target = o_ref.at[c * devices + me]
                if ka or kb:
                    pltpu.make_async_remote_copy(
                        src_ref=source,
                        dst_ref=target,
                        send_sem=send_sem,
                        recv_sem=recv_sem,
                        device_id=(a, b),
                        device_id_type=MESH,
                    ).start()
                else:
                    pltpu.make_async_copy(source, target, local_sem).start()
        return carry

    lax.fori_loop(0, parts, one_part, 0)
    remote = pl.ds(0, parts * (devices - 1))
    pltpu.make_async_copy(held.at[remote], held.at[remote], send_sem).wait()
    pltpu.make_async_copy(o_ref.at[remote], o_ref.at[remote], recv_sem).wait()
    own = pl.ds(0, parts)
    pltpu.make_async_copy(held.at[own], o_ref.at[own], local_sem).wait()


def on_device(
    rads,
    modes,
    coefficients,
    legendre,
    radial_left_factor,
    radial_right,
    eigen_rates,
    diffusivity,
    slot_order,
    slot_start,
):
    packed, lats = legendre.shape[2:]
    radii = radial_right.shape[1]
    fields, parts_count = coefficients.shape[:2]
    parts = fields * parts_count
    devices = rads * modes
    active_mask, degree = slot_layout(slot_order.reshape(2), slot_start.reshape(2), packed)
    degree_level = degree.astype(jnp.float32)
    harmonic = degree_level * (degree_level + 1.0) / (DEGREES * DEGREES)
    shrink = 1.0 + eigen_rates[:, :, None] + diffusivity[:, None, None] * harmonic[None, None, :]
    covered = jnp.any(active_mask, axis=0).astype(jnp.float32)
    factor = covered[None, None, :] / shrink
    arrived = lax.all_to_all(coefficients, "rad", split_axis=3, concat_axis=2, tiled=True)
    field_values = arrived.reshape(fields, parts_count, radii, packed)
    turned = jnp.einsum(
        "fkr,fcrp->fckp", radial_left_factor, field_values.astype(jnp.float32), precision=lax.Precision.HIGHEST
    )
    scaled = turned * factor[:, None]
    doubled = jnp.repeat(radial_right, 2, axis=1)
    result = jnp.einsum("ftk,fckp->fctp", doubled, scaled, precision=lax.Precision.HIGHEST)
    row_masks = jnp.tile(active_mask.astype(jnp.bfloat16), (radii, 1))
    updated = (result.astype(jnp.bfloat16) * row_masks).reshape(parts, 2 * radii, packed)
    rows, columns = radii // rads, lats // modes
    landed = pl.pallas_call(
        functools.partial(exchange_kernel, rads, modes),
        out_shape=jax.ShapeDtypeStruct((parts * devices, rows, 2, columns), jnp.bfloat16),
        in_specs=[pl.BlockSpec(memory_space=pltpu.VMEM)] * 2,
        out_specs=pl.BlockSpec(memory_space=pl.ANY),
        scratch_shapes=[
            pltpu.VMEM((parts * devices, rows, 2, columns), jnp.bfloat16),
            pltpu.SemaphoreType.DMA,
            pltpu.SemaphoreType.DMA,
            pltpu.SemaphoreType.DMA,
        ],
        compiler_params=pltpu.CompilerParams(
            collective_id=0, has_side_effects=True, vmem_limit_bytes=60 * 2**20
        ),
    )(updated, legendre.reshape(packed, lats))
    return landed.reshape(fields, parts_count, rads, modes, rows, 2, columns)


def solution(mesh):
    rads, modes = mesh.shape["rad"], mesh.shape["mode"]
    return jax.shard_map(
        functools.partial(on_device, rads, modes),
        mesh=mesh,
        in_specs=(
            P(None, None, "rad", None, "mode", None),
            P("rad", "mode", None, None),
            P(),
            P(),
            P(),
            P(),
            P("rad", "mode", None),
            P("rad", "mode", None),
        ),
        out_specs=P(None, None, None, None, "rad", None, "mode"),
        check_vma=False,
    )
```

time: 879 us -> 412 us (0.47); the launches traced: 866 us -> 411 us
  blocking collectives: 424 us -> 0 us
  local copies, waits for them, and re-layouts: 322 us -> 35.9 us
  Pallas kernels: 0 us -> 278 us
  matrix products: 31.5 us -> 17.4 us
    all_to_all x2 -> x0, blocking collectives: 424 us -> none  [the longest x1 277 us: on_device(): lax.all_to_all(sectioned, 'rad', split_axis=4, concat_axis=2, tiled=True)]
    pallas_call x0 -> x1, Pallas kernels: none -> 278 us  [on_device(): pl.pallas_call(functools.partial(exchange_kernel, rads, modes), out_shape...]
    all_to_all x3 -> x0, local copies, waits for them, and re-layouts: 154 us -> none  [the longest x2 77.7 us: on_device(): lax.all_to_all(lax.all_to_all(sectioned, 'rad', split_axis=4, concat_axis...]
    unnamed x23 -> x14, local copies, waits for them, and re-layouts: 130 us -> 16.2 us
    another operation x2 -> x3, local copies, waits for them, and re-layouts: 35.8 us -> 1.72 us  [on_device(): row_masks = jnp.tile(active_mask.astype(jnp.bfloat16), (radii, 1))]
    dot_general x13 -> x2, matrix products: 31.5 us -> 17.4 us  [the longest x1 13.3 us: on_device(): jnp.einsum('ftk,fckp->fctp', doubled, scaled, precision=lax.Precision.HIG...]
    mul x0 -> x1, local copies, waits for them, and re-layouts: none -> 10.3 us  [on_device(): result.astype(jnp.bfloat16) * row_masks]
  transfers between devices with their start and end apart: 1 -> 1, of which waited for: 1 -> 1; matrix products, arithmetic and copies ran while one was open for 1% -> 3% of each run, Pallas kernels for 0% -> 0%
where the time goes in v1:
time: 412 us; the launch traced here: 411 us
  Pallas kernels  278 us (67%)
  waiting for transfers between devices  67.2 us (16%)
  local copies, waits for them, and re-layouts  35.9 us (9%)
  matrix products  17.4 us (4%)
  starting transfers between devices  7.44 us (2%)
  other arithmetic  4.58 us (1%)
    pallas_call x1, Pallas kernels, on_device(): pl.pallas_call(functools.partial(exchange_kernel, rads, modes), out_shape...  278 us
    all_to_all x1, waiting for transfers between devices, on_device(): lax.all_to_all(coefficients, 'rad', split_axis=3, concat_axis=2, tiled=True)  67.2 us
    unnamed x14, local copies, waits for them, and re-layouts  16.2 us
    dot_general x1, matrix products, on_device(): jnp.einsum('ftk,fckp->fctp', doubled, scaled, precision=lax.Precision.HIG...  13.3 us
    mul x1, local copies, waits for them, and re-layouts, on_device(): result.astype(jnp.bfloat16) * row_masks  10.3 us
  transfers between devices with their start and end apart: 1, of which 1 were waited for; matrix products, arithmetic and copies ran while one was open for 3% of the time, Pallas kernels for 0%

profile of v1, /device:TPU:0, one launch (start us, length us, event | category | flops | bytes accessed | tf_op | source)
XLA Modules:
  0.0 410.5 jit_solution(16306407680807805404)
XLA Ops:
  0.0 0.0 copy-start
  0.0 4.4 %copy.13 = bf16[3,2,32,8,1,1152]{5,2,1,0,4,3:T(8,128)(2,1)} copy(bf16[3,2,32,8,1,1152]{5,3,4,2,1,0:T(8,128)(2,1)} %param.8) | data formatting | bytes 7077888 | tf_op args[0]
  4.4 0.0 copy-start.3
  4.4 0.0 copy-start.5
  4.5 7.4 %all-to-all-start = ((bf16[3,2,32,8,1,1152]{5,2,1,0,4,3:T(8,128)(2,1)}), bf16[3,2,32,8,1,1152]{5,2,1,0,4,3:T(8,128)(2,1)}, u32[]{:S(2)}, u32[]{:S(2)}) async-start(bf16[3,2,32,8,1,1152]{5,2,1,0,4,3:T(8,128)(2,1)} %copy.13), calls=%async_computation | async-start | bytes 7077888 | tf_op jit(solution)/shard_map/all_to_all | solution.py:103
  11.9 0.0 copy-done.3
  11.9 0.0 copy-done.5
  11.9 0.0 copy-start.4
  11.9 0.1 fusion.7
  12.1 0.4 copy-done.4
  12.5 0.6 tile.8
  13.1 0.5 tile.9
  13.6 0.6 copy.16
  14.2 2.9 broadcast_in_dim.7
  17.1 2.4 reshape.208
  19.5 0.8 select_reduce_fusion
  20.2 0.7 broadcast_add_fusion
  20.9 0.7 broadcast_multiply_fusion
  21.6 2.3 add_divide_fusion
  23.9 67.2 %all-to-all-done = bf16[3,2,32,8,1,1152]{5,2,1,0,4,3:T(8,128)(2,1)} async-done(((bf16[3,2,32,8,1,1152]{5,2,1,0,4,3:T(8,128)(2,1)}), bf16[3,2,32,8,1,1152]{5,2,1,0,4,3:T(8,128)(2,1)}, u32[]{:S(2)}, u32[]{:S(2)}) %all-to-all-start) | async-done | bytes 3538976 | tf_op jit(solution)/shard_map/all_to_all | solution.py:103
  91.1 2.4 copy.14
  93.5 0.0 copy-done
  93.5 0.0 copy-start.2
  93.5 4.1 fusion.3
  97.6 0.0 copy-done.2
  97.7 13.3 %bitcast_multiply_fusion = bf16[3,2,512,1152]{2,3,1,0:T(8,128)(2,1)} fusion(f32[3,2,1152,256]{3,2,1,0:T(8,128)S(1)} %fusion.3, bf16[512,1152]{0,1:T(8,128)(2,1)S(1)} %copy.16, f32[3,256,1152]{1,2,0:T(8,128)S(1)} %copy-done.2, f32[3,512,256,1]{2,1,0,3:T(8,128)S(1)} %reshape.208), kind=kOutput, calls=%fused_computation | convolution fusion | flops 10880483328 | bytes 20447232 | tf_op jit(solution)/shard_map/ftk,fckp->fctp/dot_general | solution.py:110
  111.0 10.3 %copy.17 = bf16[3,2,512,1152]{3,2,1,0:T(8,128)(2,1)} copy(bf16[3,2,512,1152]{2,3,1,0:T(8,128)(2,1)} %bitcast_multiply_fusion) | data formatting | bytes 14155776 | tf_op jit(solution)/shard_map/mul | solution.py:112
  121.3 277.7 %shard_map.82 = bf16[192,32,2,512]{3,2,1,0:T(2,128)(2,1)} custom-call(bf16[6,512,1152]{2,1,0:T(8,128)(2,1)} %bitcast.30, bf16[1152,2048]{1,0:T(8,128)(2,1)} %bitcast.32), custom_call_target="tpu_custom_call" | custom-call | tf_op jit(solution)/shard_map/pallas_call | solution.py:114
  399.0 0.0 copy-start.1
  399.0 11.3 %copy.22 = bf16[3,2,8,4,32,2,512]{6,5,4,3,2,1,0:T(2,128)(2,1)} copy(bf16[3,2,8,4,32,2,512]{6,5,4,3,2,1,0:T(2,128)(2,1)} %bitcast.29) | data formatting | bytes 25165824
  410.4 0.0 copy-done.1
  (4 shorter events, 0.0 us)
Async XLA Ops:
  0.0 93.5 %copy-start = (f32[3,256,256]{2,1,0:T(8,128)S(1)}, f32[3,256,256]{2,1,0:T(8,128)}, u32[]{:S(2)}) copy-start(f32[3,256,256]{2,1,0:T(8,128)} %param.10) | copy-start | bytes 2359300
  4.4 7.4 %copy-start.3 = (s32[1,1,2]{2,1,0:T(1,128)S(1)}, s32[1,1,2]{2,1,0:T(1,128)}, u32[]{:S(2)}) copy-start(s32[1,1,2]{2,1,0:T(1,128)} %param.15) | copy-start | bytes 28
  4.4 7.5 %copy-start.5 = (s32[1,1,2]{2,1,0:T(1,128)S(1)}, s32[1,1,2]{2,1,0:T(1,128)}, u32[]{:S(2)}) copy-start(s32[1,1,2]{2,1,0:T(1,128)} %param.14) | copy-start | bytes 28
  4.5 86.7 %all-to-all-start = ((bf16[3,2,32,8,1,1152]{5,2,1,0,4,3:T(8,128)(2,1)}), bf16[3,2,32,8,1,1152]{5,2,1,0,4,3:T(8,128)(2,1)}, u32[]{:S(2)}, u32[]{:S(2)}) async-start(bf16[3,2,32,8,1,1152]{5,2,1,0,4,3:T(8,128)(2,1)} %copy.13), calls=%async_computation | async-start | bytes 7077888 | tf_op jit(solution)/shard_map/all_to_all | solution.py:103
  11.9 0.6 copy-start.4
  93.5 4.1 %copy-start.2 = (f32[3,256,1152]{1,2,0:T(8,128)S(1)}, f32[3,256,1152]{1,2,0:T(8,128)}, u32[]{:S(2)}) copy-start(f32[3,256,1152]{1,2,0:T(8,128)} %add_divide_fusion) | copy-start | bytes 10616836
  399.0 11.4 %copy-start.1 = (f32[3,256,256]{2,1,0:T(8,128)S(1)}, f32[3,256,256]{2,1,0:T(8,128)}, u32[]{:S(2)}) copy-start(f32[3,256,256]{2,1,0:T(8,128)} %param.10) | copy-start | bytes 2359300

commit v2 on v1

v2 whole, which is shorter than its diff:
```python
import functools
import jax
import jax.numpy as jnp
from jax import lax
from jax.experimental import pallas as pl
from jax.experimental.pallas import tpu as pltpu
from jax.sharding import PartitionSpec as P

DEGREES = 1024
BLOCK = 128
MESH = pl.DeviceIdType.MESH


def far_first(count):
    return sorted(range(count), key=lambda k: (-min(k, count - k), k))


def whole_kernel(
    rads,
    modes,
    parts_count,
    order_ref,
    start_ref,
    diffusivity_ref,
    eigen_ref,
    left_ref,
    right_ref,
    x_ref,
    legendre_ref,
    o_ref,
    arrived,
    polynomial_rows,
    updated,
    held,
    in_send,
    in_recv,
    legendre_sem,
    out_send,
    out_recv,
    out_local,
):
    my_rad = lax.axis_index("rad")
    my_mode = lax.axis_index("mode")
    devices = rads * modes
    parts = arrived.shape[0]
    packed = arrived.shape[3]
    radii = right_ref.shape[1]
    rows, lats = held.shape[1], held.shape[3]
    me = my_rad * modes + my_mode

    fetch = pltpu.make_async_copy(legendre_ref, polynomial_rows, legendre_sem)
    fetch.start()
    barrier = pltpu.get_barrier_semaphore()
    for ka in range(rads):
        for kb in range(modes):
            if ka or kb:
                peer = (lax.rem(my_rad + ka, rads), lax.rem(my_mode + kb, modes))
                pl.semaphore_signal(barrier, inc=1, device_id=peer, device_id_type=MESH)
    pl.semaphore_wait(barrier, devices - 1)

    def send_part(c, carry):
        for ka in far_first(rads):
            a = lax.rem(my_rad + ka, rads)
            source = x_ref.at[a, c]
            target = arrived.at[c, my_rad]
            if ka:
                pltpu.make_async_remote_copy(
                    src_ref=source,
                    dst_ref=target,
                    send_sem=in_send,
                    recv_sem=in_recv.at[c],
                    device_id=(a, my_mode),
                    device_id_type=MESH,
                ).start()
            else:
                pltpu.make_async_copy(source, target, in_recv.at[c]).start()
        return carry

    lax.fori_loop(0, parts, send_part, 0)

    position = lax.broadcasted_iota(jnp.int32, (1, packed), 1)
    live = []
    degree = jnp.zeros((1, packed), jnp.int32)
    for s in range(2):
        order = order_ref[0, 0, s]
        start = start_ref[0, 0, s]
        first_degree = BLOCK * (order // BLOCK)
        inside = (position >= start) & (position < start + DEGREES - first_degree)
        row_degree = first_degree + position - start
        degree = degree + jnp.where(inside, row_degree, 0)
        live.append(jnp.where(inside & (row_degree >= order), 1.0, 0.0).astype(jnp.float32))
    degree_level = degree.astype(jnp.float32)
    harmonic = degree_level * (degree_level + 1.0) / (DEGREES * DEGREES)
    covered = jnp.maximum(live[0], live[1])
    row = lax.broadcasted_iota(jnp.int32, (2 * radii, radii), 0)
    column = lax.broadcasted_iota(jnp.int32, (2 * radii, radii), 1)
    doubling = jnp.where(row // 2 == column, 1.0, 0.0).astype(jnp.bfloat16)
    parity = lax.broadcasted_iota(jnp.int32, (2 * radii, packed), 0) % 2
    fetch.wait()

    def one_part(c, carry):
        field = c // parts_count
        pltpu.make_async_copy(arrived.at[c], arrived.at[c], in_recv.at[c]).wait()
        rates = eigen_ref[pl.ds(field, 1), :]
        rates = jnp.transpose(jnp.broadcast_to(rates, (128, radii)))[:, 0:1]
        shrink = 1.0 + rates + diffusivity_ref[field] * harmonic
        values = arrived[c].reshape(radii, packed).astype(jnp.float32)
        turned = jnp.dot(
            left_ref[field], values, precision=lax.Precision.HIGHEST, preferred_element_type=jnp.float32
        )
        scaled = turned * (covered / shrink)
        result = jnp.dot(
            right_ref[field], scaled, precision=lax.Precision.HIGHEST, preferred_element_type=jnp.float32
        )
        doubled = jnp.dot(doubling, result.astype(jnp.bfloat16), preferred_element_type=jnp.float32)
        updated[...] = (doubled * jnp.where(parity == 0, live[0], live[1])).astype(jnp.bfloat16)
        for kb in range(modes):
            b = lax.rem(my_mode + kb, modes)
            columns = pl.ds(pl.multiple_of(b * lats, lats), lats)
            summed = jnp.dot(
                updated[...], polynomial_rows[:, columns], preferred_element_type=jnp.float32
            )
            blocks = summed.reshape(rads, rows, 2, lats).astype(jnp.bfloat16)
            for a in range(rads):
                held[(c * modes + kb) * rads + a] = blocks[a]
            for ka in far_first(rads):
                a = lax.rem(my_rad + ka, rads)
                source = held.at[(c * modes + kb) * rads + a]
                target = o_ref.at[c * devices + me]
                if ka or kb:
                    pltpu.make_async_remote_copy(
                        src_ref=source,
                        dst_ref=target,
                        send_sem=out_send,
                        recv_sem=out_recv,
                        device_id=(a, b),
                        device_id_type=MESH,
                    ).start()
                else:
                    pltpu.make_async_copy(source, target, out_local).start()
        return carry

    lax.fori_loop(0, parts, one_part, 0)
    others = arrived.at[:, pl.ds(0, rads - 1)]
    pltpu.make_async_copy(others, others, in_send).wait()
    remote = pl.ds(0, parts * (devices - 1))
    pltpu.make_async_copy(held.at[remote], held.at[remote], out_send).wait()
    pltpu.make_async_copy(o_ref.at[remote], o_ref.at[remote], out_recv).wait()
    own = pl.ds(0, parts)
    pltpu.make_async_copy(held.at[own], o_ref.at[own], out_local).wait()


def on_device(
    rads,
    modes,
    coefficients,
    legendre,
    radial_left_factor,
    radial_right,
    eigen_rates,
    diffusivity,
    slot_order,
    slot_start,
):
    packed, lats = legendre.shape[2:]
    radii = radial_right.shape[1]
    fields, parts_count = coefficients.shape[:2]
    parts = fields * parts_count
    devices = rads * modes
    rows, columns = radii // rads, lats // modes
    outgoing = jnp.transpose(
        coefficients.reshape(parts, rows, rads, packed), (2, 0, 1, 3)
    )
    smem = pl.BlockSpec(memory_space=pltpu.SMEM)
    vmem = pl.BlockSpec(memory_space=pltpu.VMEM)
    hbm = pl.BlockSpec(memory_space=pltpu.HBM)
    landed = pl.pallas_call(
        functools.partial(whole_kernel, rads, modes, parts_count),
        out_shape=jax.ShapeDtypeStruct((parts * devices, rows, 2, columns), jnp.bfloat16),
        in_specs=[smem, smem, smem, vmem, vmem, vmem, hbm, hbm],
        out_specs=pl.BlockSpec(memory_space=pl.ANY),
        scratch_shapes=[
            pltpu.VMEM((parts, rads, rows, packed), jnp.bfloat16),
            pltpu.VMEM((packed, lats), jnp.bfloat16),
            pltpu.VMEM((2 * radii, packed), jnp.bfloat16),
            pltpu.VMEM((parts * devices, rows, 2, columns), jnp.bfloat16),
            pltpu.SemaphoreType.DMA,
            pltpu.SemaphoreType.DMA((parts,)),
            pltpu.SemaphoreType.DMA,
            pltpu.SemaphoreType.DMA,
            pltpu.SemaphoreType.DMA,
            pltpu.SemaphoreType.DMA,
        ],
        compiler_params=pltpu.CompilerParams(
            collective_id=0, has_side_effects=True, vmem_limit_bytes=40 * 2**20
        ),
    )(
        slot_order,
        slot_start,
        diffusivity,
        eigen_rates,
        radial_left_factor,
        radial_right,
        outgoing,
        legendre.reshape(packed, lats),
    )
    return landed.reshape(fields, parts_count, rads, modes, rows, 2, columns)


def solution(mesh):
    rads, modes = mesh.shape["rad"], mesh.shape["mode"]
    return jax.shard_map(
        functools.partial(on_device, rads, modes),
        mesh=mesh,
        in_specs=(
            P(None, None, "rad", None, "mode", None),
            P("rad", "mode", None, None),
            P(),
            P(),
            P(),
            P(),
            P("rad", "mode", None),
            P("rad", "mode", None),
        ),
        out_specs=P(None, None, None, None, "rad", None, "mode"),
        check_vma=False,
    )
```

time: 412 us -> 371 us (0.900)
  Pallas kernels: 278 us -> 354 us
  waiting for transfers between devices: 67.2 us -> 0 us
  local copies, waits for them, and re-layouts: 35.9 us -> 15.1 us
  matrix products: 17.4 us -> 0 us
  starting transfers between devices: 7.44 us -> 0 us
  other arithmetic: 4.58 us -> 0 us
    pallas_call x1, Pallas kernels: 278 us -> 354 us  [on_device(): pl.pallas_call(functools.partial(whole_kernel, rads, modes, parts_count),...]
    all_to_all x1 -> x0, waiting for transfers between devices: 67.2 us -> none  [on_device(): lax.all_to_all(coefficients, 'rad', split_axis=3, concat_axis=2, tiled=True)]
    dot_general x2 -> x0, matrix products: 17.4 us -> none  [the longest x1 13.3 us: on_device(): jnp.einsum('ftk,fckp->fctp', doubled, scaled, precision=lax.Precision.HIG...]
    mul x1 -> x0, local copies, waits for them, and re-layouts: 10.3 us -> none  [on_device(): result.astype(jnp.bfloat16) * row_masks]
    all_to_all x1 -> x0, starting transfers between devices: 7.44 us -> none  [on_device(): lax.all_to_all(coefficients, 'rad', split_axis=3, concat_axis=2, tiled=True)]
    unnamed x14 -> x16, local copies, waits for them, and re-layouts: 16.2 us -> 15.1 us
  transfers between devices with their start and end apart: 1 -> 0, of which waited for: 1 -> 0; matrix products, arithmetic and copies ran while one was open for 3% -> 0% of each run, Pallas kernels for 0% -> 0%
where the time goes in v2:
time: 371 us; the launch traced here: 370 us
  Pallas kernels  354 us (95%)
  local copies, waits for them, and re-layouts  15.1 us (4%)
    pallas_call x1, Pallas kernels, on_device(): pl.pallas_call(functools.partial(whole_kernel, rads, modes, parts_count),...  354 us
    unnamed x16, local copies, waits for them, and re-layouts  15.1 us

profile of v2, /device:TPU:0, one launch (start us, length us, event | category | flops | bytes accessed | tf_op | source)
XLA Modules:
  0.0 369.6 jit_solution(14315428530125153689)
XLA Ops:
  0.0 0.0 copy-start.5
  0.0 0.0 copy-start.4
  0.0 0.0 copy-start.6
  0.0 0.0 copy-start.3
  0.0 0.0 copy-start.2
  0.0 0.0 copy-start.1
  0.0 0.0 copy-start
  0.0 2.7 copy.9
  2.8 0.0 copy-done.5
  2.8 0.0 copy-done.4
  2.8 0.0 copy-done.6
  2.8 0.0 copy-done.3
  2.8 0.0 copy-done.2
  2.8 0.0 copy-done.1
  2.8 1.1 copy-done
  3.9 354.4 %shard_map.82 = bf16[192,32,2,512]{3,2,1,0:T(2,128)(2,1)} custom-call(s32[1,1,2]{2,1,0:T(1,128)S(1)} %copy-done.4, s32[1,1,2]{2,1,0:T(1,128)S(1)} %copy-done.5, f32[3]{0:T(128)S(1)} %copy-done.6, f32[3,256]{1,0:T(4,128)S(1)} %copy-done.3, f32[3,256,256]{2,1,0:T(8,128)S(1)} %copy-done.1, f32[3,256,256]{2,1,0:T(8,128)S(1)} %copy-done.2, ...), custom_call_target="tpu_custom_call" | custom-call | tf_op jit(solution)/shard_map/pallas_call | solution.py:177
  358.3 11.3 %copy.11 = bf16[3,2,8,4,32,2,512]{6,5,4,3,2,1,0:T(2,128)(2,1)} copy(bf16[3,2,8,4,32,2,512]{6,5,4,3,2,1,0:T(2,128)(2,1)} %bitcast.7) | data formatting | bytes 25165824
Async XLA Ops:
  0.0 2.8 copy-start.5
  0.0 2.8 copy-start.4
  0.0 2.8 copy-start.6
  0.0 2.8 copy-start.3
  0.0 2.8 copy-start.2
  0.0 2.8 copy-start.1
  0.0 3.9 %copy-start = (bf16[1,1,1152,2048]{3,2,1,0:T(8,128)(2,1)S(1)}, bf16[1,1,1152,2048]{3,2,1,0:T(8,128)(2,1)}, u32[]{:S(2)}) copy-start(bf16[1,1,1152,2048]{3,2,1,0:T(8,128)(2,1)} %param.9) | copy-start | bytes 14155780

commit v3 on v2

--- a/solution.py
+++ b/solution.py
@@ -23,17 +23,23 @@
     start_ref,
     diffusivity_ref,
     eigen_ref,
-    left_ref,
-    right_ref,
+    left_hbm,
+    right_hbm,
     x_ref,
     legendre_ref,
     o_ref,
+    left_ref,
+    right_ref,
+    entering,
+    outgoing,
     arrived,
     polynomial_rows,
     updated,
     held,
+    enter_sem,
     in_send,
     in_recv,
+    factor_sem,
     legendre_sem,
     out_send,
     out_recv,
@@ -48,20 +54,40 @@
     rows, lats = held.shape[1], held.shape[3]
     me = my_rad * modes + my_mode
 
-    fetch = pltpu.make_async_copy(legendre_ref, polynomial_rows, legendre_sem)
-    fetch.start()
+    def enter(c):
+        return pltpu.make_async_copy(x_ref.at[c], entering.at[c], enter_sem.at[c])
+
+    for c in range(parts):
+        enter(c).start()
+    fetches = (
+        pltpu.make_async_copy(left_hbm, left_ref, factor_sem.at[0]),
+        pltpu.make_async_copy(right_hbm, right_ref, factor_sem.at[1]),
+        pltpu.make_async_copy(legendre_ref, polynomial_rows, legendre_sem),
+    )
+    for fetch in fetches:
+        fetch.start()
     barrier = pltpu.get_barrier_semaphore()
     for ka in range(rads):
         for kb in range(modes):
             if ka or kb:
                 peer = (lax.rem(my_rad + ka, rads), lax.rem(my_mode + kb, modes))
                 pl.semaphore_signal(barrier, inc=1, device_id=peer, device_id_type=MESH)
+
+    def turn(c):
+        enter(c).wait()
+        outgoing[c] = jnp.swapaxes(entering[c], 0, 1)
+
+    turn(0)
     pl.semaphore_wait(barrier, devices - 1)
 
     def send_part(c, carry):
+        @pl.when(c > 0)
+        def _():
+            turn(c)
+
         for ka in far_first(rads):
             a = lax.rem(my_rad + ka, rads)
-            source = x_ref.at[a, c]
+            source = outgoing.at[c, a]
             target = arrived.at[c, my_rad]
             if ka:
                 pltpu.make_async_remote_copy(
@@ -96,7 +122,8 @@
     column = lax.broadcasted_iota(jnp.int32, (2 * radii, radii), 1)
     doubling = jnp.where(row // 2 == column, 1.0, 0.0).astype(jnp.bfloat16)
     parity = lax.broadcasted_iota(jnp.int32, (2 * radii, packed), 0) % 2
-    fetch.wait()
+    for fetch in fetches:
+        fetch.wait()
 
     def one_part(c, carry):
         field = c // parts_count
@@ -168,31 +195,34 @@
     parts = fields * parts_count
     devices = rads * modes
     rows, columns = radii // rads, lats // modes
-    outgoing = jnp.transpose(
-        coefficients.reshape(parts, rows, rads, packed), (2, 0, 1, 3)
-    )
     smem = pl.BlockSpec(memory_space=pltpu.SMEM)
     vmem = pl.BlockSpec(memory_space=pltpu.VMEM)
     hbm = pl.BlockSpec(memory_space=pltpu.HBM)
     landed = pl.pallas_call(
         functools.partial(whole_kernel, rads, modes, parts_count),
-        out_shape=jax.ShapeDtypeStruct((parts * devices, rows, 2, columns), jnp.bfloat16),
-        in_specs=[smem, smem, smem, vmem, vmem, vmem, hbm, hbm],
+        out_shape=pltpu.VMEM((parts * devices, rows, 2, columns), jnp.bfloat16),
+        in_specs=[smem, smem, smem, vmem, hbm, hbm, hbm, hbm],
         out_specs=pl.BlockSpec(memory_space=pl.ANY),
         scratch_shapes=[
+            pltpu.VMEM(radial_left_factor.shape, jnp.float32),
+            pltpu.VMEM(radial_right.shape, jnp.float32),
+            pltpu.VMEM((parts, rows, rads, packed), jnp.bfloat16),
+            pltpu.VMEM((parts, rads, rows, packed), jnp.bfloat16),
             pltpu.VMEM((parts, rads, rows, packed), jnp.bfloat16),
             pltpu.VMEM((packed, lats), jnp.bfloat16),
             pltpu.VMEM((2 * radii, packed), jnp.bfloat16),
             pltpu.VMEM((parts * devices, rows, 2, columns), jnp.bfloat16),
-            pltpu.SemaphoreType.DMA,
             pltpu.SemaphoreType.DMA((parts,)),
+            pltpu.SemaphoreType.DMA,
+            pltpu.SemaphoreType.DMA((parts,)),
+            pltpu.SemaphoreType.DMA((2,)),
             pltpu.SemaphoreType.DMA,
             pltpu.SemaphoreType.DMA,
             pltpu.SemaphoreType.DMA,
             pltpu.SemaphoreType.DMA,
         ],
         compiler_params=pltpu.CompilerParams(
-            collective_id=0, has_side_effects=True, vmem_limit_bytes=40 * 2**20
+            collective_id=0, has_side_effects=True, vmem_limit_bytes=46 * 2**20
         ),
     )(
         slot_order,
@@ -201,7 +231,7 @@
         eigen_rates,
         radial_left_factor,
         radial_right,
-        outgoing,
+        coefficients.reshape(parts, rows, rads, packed),
         legendre.reshape(packed, lats),
     )
     return landed.reshape(fields, parts_count, rads, modes, rows, 2, columns)

time: 371 us -> 360 us (0.970)
  local copies, waits for them, and re-layouts: 15.1 us -> 4.78 us
    unnamed x16 -> x1, local copies, waits for them, and re-layouts: 15.1 us -> 4.78 us
where the time goes in v3:
time: 360 us; the launch traced here: 359 us
  Pallas kernels  354 us (98%)
  local copies, waits for them, and re-layouts  4.78 us (1%)
    pallas_call x1, Pallas kernels, on_device(): pl.pallas_call(functools.partial(whole_kernel, rads, modes, parts_count),...  354 us

profile of v3, /device:TPU:0, one launch (start us, length us, event | category | flops | bytes accessed | tf_op | source)
XLA Modules:
  0.0 358.9 jit_solution(7620714283054562538)
XLA Ops:
  0.0 354.2 %shard_map.82 = bf16[192,32,2,512]{3,2,1,0:T(2,128)(2,1)S(1)} custom-call(s32[1,1,2]{2,1,0:T(1,128)} %order_ref.1, s32[1,1,2]{2,1,0:T(1,128)} %start_ref.1, f32[3]{0:T(128)} %diffusivity_ref.1, f32[3,256]{1,0:T(4,128)} %eigen_ref.1, f32[3,256,256]{2,1,0:T(8,128)} %left_hbm.1, f32[3,256,256]{2,1,0:T(8,128)} %right_hbm.1, bf16[6,32,8,1152]{3,2,1,0:T(8,128)(2,1)} %bitcast.5, ...), custom_call_target="tpu_custom_call" | custom-call | tf_op jit(solution)/shard_map/pallas_call | solution.py:201
  354.2 4.8 %copy.10 = bf16[3,2,8,4,32,2,512]{6,5,4,3,2,1,0:T(2,128)(2,1)} copy(bf16[3,2,8,4,32,2,512]{6,5,4,3,2,1,0:T(2,128)(2,1)S(1)} %bitcast.3) | data formatting | bytes 25165824

commit v4 on v3

--- a/solution.py
+++ b/solution.py
@@ -11,8 +11,11 @@
 MESH = pl.DeviceIdType.MESH
 
 
-def far_first(count):
-    return sorted(range(count), key=lambda k: (-min(k, count - k), k))
+def peer_rad(my_rad, rads, k):
+    half = rads // 2
+    near = my_rad // half
+    side = near if k < half else 1 - near
+    return side * half + lax.rem(my_rad % half + k, half)
 
 
 def whole_kernel(
@@ -85,8 +88,8 @@
         def _():
             turn(c)
 
-        for ka in far_first(rads):
-            a = lax.rem(my_rad + ka, rads)
+        for ka in range(rads):
+            a = peer_rad(my_rad, rads, ka)
             source = outgoing.at[c, a]
             target = arrived.at[c, my_rad]
             if ka:
@@ -150,8 +153,10 @@
             blocks = summed.reshape(rads, rows, 2, lats).astype(jnp.bfloat16)
             for a in range(rads):
                 held[(c * modes + kb) * rads + a] = blocks[a]
-            for ka in far_first(rads):
-                a = lax.rem(my_rad + ka, rads)
+        for ka in range(rads):
+            for kb in range(modes):
+                a = peer_rad(my_rad, rads, ka)
+                b = lax.rem(my_mode + kb, modes)
                 source = held.at[(c * modes + kb) * rads + a]
                 target = o_ref.at[c * devices + me]
                 if ka or kb:

time: 360 us -> 368 us (1.022)
  Pallas kernels: 354 us -> 363 us
    pallas_call x1, Pallas kernels: 354 us -> 363 us  [on_device(): pl.pallas_call(functools.partial(whole_kernel, rads, modes, parts_count),...]
where the time goes in v4:
time: 368 us; the launch traced here: 367 us
  Pallas kernels  363 us (99%)
  local copies, waits for them, and re-layouts  4.78 us (1%)
    pallas_call x1, Pallas kernels, on_device(): pl.pallas_call(functools.partial(whole_kernel, rads, modes, parts_count),...  363 us

profile of v4, /device:TPU:0, one launch (start us, length us, event | category | flops | bytes accessed | tf_op | source)
XLA Modules:
  0.0 367.4 jit_solution(6847164562789972152)
XLA Ops:
  0.0 362.7 %shard_map.82 = bf16[192,32,2,512]{3,2,1,0:T(2,128)(2,1)S(1)} custom-call(s32[1,1,2]{2,1,0:T(1,128)} %order_ref.1, s32[1,1,2]{2,1,0:T(1,128)} %start_ref.1, f32[3]{0:T(128)} %diffusivity_ref.1, f32[3,256]{1,0:T(4,128)} %eigen_ref.1, f32[3,256,256]{2,1,0:T(8,128)} %left_hbm.1, f32[3,256,256]{2,1,0:T(8,128)} %right_hbm.1, bf16[6,32,8,1152]{3,2,1,0:T(8,128)(2,1)} %bitcast.5, ...), custom_call_target="tpu_custom_call" | custom-call | tf_op jit(solution)/shard_map/pallas_call | solution.py:206
  362.7 4.8 %copy.10 = bf16[3,2,8,4,32,2,512]{6,5,4,3,2,1,0:T(2,128)(2,1)} copy(bf16[3,2,8,4,32,2,512]{6,5,4,3,2,1,0:T(2,128)(2,1)S(1)} %bitcast.3) | data formatting | bytes 25165824

commit v5 on v4

--- a/solution.py
+++ b/solution.py
@@ -88,7 +88,7 @@
         def _():
             turn(c)
 
-        for ka in range(rads):
+        for ka in reversed(range(rads)):
             a = peer_rad(my_rad, rads, ka)
             source = outgoing.at[c, a]
             target = arrived.at[c, my_rad]
@@ -153,10 +153,8 @@
             blocks = summed.reshape(rads, rows, 2, lats).astype(jnp.bfloat16)
             for a in range(rads):
                 held[(c * modes + kb) * rads + a] = blocks[a]
-        for ka in range(rads):
-            for kb in range(modes):
+            for ka in reversed(range(rads)):
                 a = peer_rad(my_rad, rads, ka)
-                b = lax.rem(my_mode + kb, modes)
                 source = held.at[(c * modes + kb) * rads + a]
                 target = o_ref.at[c * devices + me]
                 if ka or kb:

time: 368 us -> 364 us (0.989)
  Pallas kernels: 363 us -> 359 us
    pallas_call x1, Pallas kernels: 363 us -> 359 us  [on_device(): pl.pallas_call(functools.partial(whole_kernel, rads, modes, parts_count),...]
where the time goes in v5:
time: 364 us; the launch traced here: 363 us
  Pallas kernels  359 us (99%)
  local copies, waits for them, and re-layouts  4.78 us (1%)
    pallas_call x1, Pallas kernels, on_device(): pl.pallas_call(functools.partial(whole_kernel, rads, modes, parts_count),...  359 us

profile of v5, /device:TPU:0, one launch (start us, length us, event | category | flops | bytes accessed | tf_op | source)
XLA Modules:
  0.0 363.4 jit_solution(11843879531381236528)
XLA Ops:
  0.0 358.6 %shard_map.82 = bf16[192,32,2,512]{3,2,1,0:T(2,128)(2,1)S(1)} custom-call(s32[1,1,2]{2,1,0:T(1,128)} %order_ref.1, s32[1,1,2]{2,1,0:T(1,128)} %start_ref.1, f32[3]{0:T(128)} %diffusivity_ref.1, f32[3,256]{1,0:T(4,128)} %eigen_ref.1, f32[3,256,256]{2,1,0:T(8,128)} %left_hbm.1, f32[3,256,256]{2,1,0:T(8,128)} %right_hbm.1, bf16[6,32,8,1152]{3,2,1,0:T(8,128)(2,1)} %bitcast.5, ...), custom_call_target="tpu_custom_call" | custom-call | tf_op jit(solution)/shard_map/pallas_call | solution.py:204
  358.6 4.8 %copy.10 = bf16[3,2,8,4,32,2,512]{6,5,4,3,2,1,0:T(2,128)(2,1)} copy(bf16[3,2,8,4,32,2,512]{6,5,4,3,2,1,0:T(2,128)(2,1)S(1)} %bitcast.3) | data formatting | bytes 25165824
